TPU v7x, 512 devices: a whole 4x4x16 slice. The times are simulated.
512 devices in a mesh: mp: 2 (over y_hi), tok: 8 (over x, core), lat: 32 (over z, y_lo).
Axes of the slice: x: 4, y: 4 (y_hi: 2, y_lo: 2; y = y_hi * 2 + y_lo), z: 16, core: 2. Of those that a mesh axis runs over, the one named last changes fastest.
Arguments:
- inputs: bfloat16 [2, 384, 4608], P('mp', 'lat', 'tok'), may hold values from -6 to 6
- gate_w: bfloat16 [2, 4608, 18432], P('mp', 'tok', 'lat'), may hold values from -0.09375 to 0.09375
- up_w: bfloat16 [2, 4608, 18432], P('mp', 'tok', 'lat'), may hold values from -0.09375 to 0.09375
- down_w: bfloat16 [2, 18432, 4608], P('mp', 'lat', 'tok'), may hold values from -0.046875 to 0.046875
- enc_w: bfloat16 [2, 4608, 8192], P('mp', 'tok', 'lat'), may hold values from -0.0625 to 0.0625
- enc_bias: float32 [8192], P('lat'), may hold values from -3 to 3
- dec_w: bfloat16 [8192, 2, 4608], P('lat', 'mp', 'tok'), may hold values from -0.0625 to 0.0625
- dec_bias: float32 [2, 4608], P('mp', 'tok'), may hold values from -3 to 3
Outputs:
- recon_error: float32 [2, 384, 4608], P('mp', 'lat', 'tok')
- dec_grad: float32 [8192, 2, 4608], P('lat', 'mp', 'tok')
- latent_grad: float32 [384, 8192], P(None, 'lat')
All inputs are finite; a program needn't handle non-finite values.
Results may differ from a plain program's by a relative error of at most 0.009.
Values may be sent and summed in bfloat16 or wider, within the bound.
A program may use at most 64 MiB of HBM per device.

v0:
```python
import jax
import jax.numpy as jnp
from jax import lax
from jax.sharding import PartitionSpec as P


def contract_rows(left, right):
    return lax.dot_general(
        left, right, (((0,), (0,)), ((), ())), preferred_element_type=jnp.float32
    )


def contract_cols(left, right):
    return lax.dot_general(
        left, right, (((1,), (1,)), ((), ())), preferred_element_type=jnp.float32
    )


def body(inputs, gate_w, up_w, down_w, enc_w, enc_bias, dec_w, dec_bias):
    x_rows = inputs[0]
    gathered = lax.all_gather(x_rows, "lat", axis=0, tiled=True)
    gate_local = gate_w[0]
    up_local = up_w[0]
    width = gate_local.shape[1]
    block = gathered
    both = lax.psum_scatter(
        jnp.concatenate(
            [
                jnp.dot(block, gate_local, preferred_element_type=jnp.float32),
                jnp.dot(block, up_local, preferred_element_type=jnp.float32),
            ],
            axis=1,
        ),
        "tok",
        scatter_dimension=0,
        tiled=True,
    )
    hidden = (jax.nn.gelu(both[:, :width], approximate=True) * both[:, width:]).astype(jnp.bfloat16)
    hidden_all = lax.all_gather(hidden, "tok", axis=0, tiled=True)
    down_local = down_w[0]
    block = hidden_all
    acts = lax.psum_scatter(
        jnp.dot(block, down_local, preferred_element_type=jnp.float32),
        "lat",
        scatter_dimension=0,
        tiled=True,
    ).astype(jnp.bfloat16)
    acts_all = lax.all_gather(acts, "lat", axis=0, tiled=True)
    partial_pre = jnp.dot(acts_all, enc_w[0], preferred_element_type=jnp.float32)
    pre = lax.psum(partial_pre, ("mp", "tok"))
    codes = jnp.maximum(pre + enc_bias, 0.0).astype(jnp.bfloat16)
    decoder = dec_w[:, 0, :]
    bias_row = dec_bias[0]
    block = codes
    recon = lax.psum_scatter(
        jnp.dot(block, decoder, preferred_element_type=jnp.float32),
        "lat",
        scatter_dimension=0,
        tiled=True,
    )
    error = recon + bias_row - acts.astype(jnp.float32)
    error_all = lax.all_gather(error.astype(jnp.bfloat16), "lat", axis=0, tiled=True)
    decoder_grad = contract_rows(codes, error_all)
    latent_grad = lax.psum(contract_cols(error_all, decoder), ("mp", "tok"))
    return (error[None], decoder_grad[:, None, :], latent_grad)


def solution(mesh):
    in_specs = (
        P("mp", "lat", "tok"),
        P("mp", "tok", "lat"),
        P("mp", "tok", "lat"),
        P("mp", "lat", "tok"),
        P("mp", "tok", "lat"),
        P("lat"),
        P("lat", "mp", "tok"),
        P("mp", "tok"),
    )
    out_specs = (P("mp", "lat", "tok"), P("lat", "mp", "tok"), P(None, "lat"))
    return jax.shard_map(body, mesh=mesh, in_specs=in_specs, out_specs=out_specs, check_vma=False)
```

profile of v0, /device:TPU:1, one launch (start us, length us, event | category | flops | bytes accessed | tf_op | source)
XLA Modules:
  0.0 789.7 jit_solution(4947730989583786598)
XLA Ops:
  7.2 0.0 copy-start
  7.2 0.0 reduce-scatter.8.cloned.1.call-start
  7.2 0.8 copy.20
  8.0 61.9 %all-gather = bf16[1,384,576]{2,0,1:T(2,128)(2,1)S(1)} all-gather(bf16[1,12,576]{2,0,1:T(2,128)(2,1)S(1)} %copy.20), channel_id=2, replica_groups=mesh['mp'=2,'tok'=8,'lat'=32] {'lat'}, dimensions={1}, use_global_device_ids=true | all-gather | bytes 456192 | tf_op jit(solution)/shard_map/all_gather | solution.py:21
  70.0 0.7 copy.21
  70.6 0.6 fusion.4
  71.3 0.6 fusion.6
  71.9 0.1 pad_maximum_fusion
  72.1 2.0 copy.25
  74.0 0.0 reduce-scatter.8.cloned.1.call-update
  74.1 0.0 all-reduce.7.cloned.1.call-start
  74.1 47.7 %reduce-scatter.8.cloned.1.call-done = f32[48,1152]{1,0:T(8,128)} async-done(((f32[384,1152]{1,0:T(8,128)}), f32[48,1152]{1,0:T(8,128)}) %reduce-scatter.8.cloned.1.call-update) | async-done | bytes 221200 | tf_op jit(solution)/shard_map/reduce_scatter | solution.py:26
  121.8 1.1 fusion.24
  122.9 15.4 %all_gather.13 = bf16[384,576]{1,0:T(8,128)(2,1)S(1)} all-gather(bf16[48,576]{1,0:T(8,128)(2,1)S(1)} %fusion.24), channel_id=1, replica_groups=mesh['mp'=2,'tok'=8,'lat'=32] {'tok'}, dimensions={0}, use_global_device_ids=true | all-gather | bytes 497664 | tf_op jit(solution)/shard_map/all_gather | solution.py:39
  138.2 0.6 fusion.2
  138.8 0.0 copy-start.5
  138.8 59.0 %fusion = f32[16,576]{1,0:T(8,128)S(1)} fusion(f32[384,576]{1,0:T(8,128)S(1)} %fusion.2), kind=kCustom, calls=%all-reduce-scatter | all-reduce-scatter fusion | flops 294913 | bytes 923648
  197.9 1.7 collective-permute-start
  199.6 2.1 collective-permute-start.1
  201.7 6.0 collective-permute-start.7
  207.7 4.9 collective-permute-start.2
  212.7 4.9 collective-permute-start.3
  217.6 0.0 collective-permute-done.7
  217.6 2.1 collective-permute-start.4
  219.8 3.5 collective-permute-start.5
  223.2 0.0 collective-permute-done.1
  223.2 2.8 collective-permute-start.6
  226.1 1.3 dynamic-slice.6
  228.0 0.0 collective-permute-done.2
  228.0 0.0 collective-permute-done.4
  228.0 0.0 collective-permute-done.5
  228.1 1.3 concatenate.4
  229.4 0.0 copy-start.2
  229.4 0.0 copy-start.6
  229.4 49.4 %all-gather.1 = bf16[32,12,576]{2,1,0:T(8,128)(2,1)S(1)} all-gather(bf16[1,12,576]{2,1,0:T(8,128)(2,1)S(1)} %fusion.31), channel_id=1, replica_groups=mesh['mp'=2,'tok'=8,'lat'=32] {'lat'}, dimensions={0}, use_global_device_ids=true | all-gather | bytes 456192 | tf_op jit(solution)/shard_map/all_gather | solution.py:48
  278.8 0.2 reshape.9
  279.1 1.1 fusion.14
  280.2 0.0 all-reduce.7.cloned.1.call-update
  280.2 0.0 all-reduce.9.cloned.1.call-start
  280.2 180.0 %all-reduce.7.cloned.1.call-done = f32[384,256]{1,0:T(8,128)} async-done(((f32[384,256]{1,0:T(8,128)}), f32[384,256]{1,0:T(8,128)}) %all-reduce.7.cloned.1.call-update) | async-done | bytes 393232 | tf_op jit(solution)/shard_map/psum | solution.py:50
  460.2 1.3 fusion.12
  461.6 59.2 %fusion.1 = f32[16,576]{1,0:T(8,128)S(1)} fusion(f32[384,576]{1,0:T(8,128)S(1)} %fusion.12), kind=kCustom, calls=%all-reduce-scatter.1 | all-reduce-scatter fusion | flops 294913 | bytes 923648
  520.7 1.3 collective-permute-start.10
  522.0 3.4 collective-permute-start.11
  525.5 7.0 collective-permute-start.15
  532.6 4.5 collective-permute-start.12
  537.1 3.9 collective-permute-start.13
  541.0 0.0 collective-permute-done.15
  541.0 2.9 collective-permute-start.14
  543.9 0.0 collective-permute-done.10
  543.9 3.1 collective-permute-start.8
  547.0 2.2 collective-permute-start.9
  549.2 0.0 collective-permute-done.12
  549.3 0.0 collective-permute-done.14
  549.3 1.0 collective-permute-done.9
  550.3 1.0 concatenate.5
  551.3 48.9 %all-gather.2 = bf16[32,12,576]{2,1,0:T(8,128)(2,1)S(1)} all-gather(bf16[1,12,576]{2,1,0:T(8,128)(2,1)S(1)} %get-tuple-element.18), channel_id=1, replica_groups=mesh['mp'=2,'tok'=8,'lat'=32] {'lat'}, dimensions={0}, use_global_device_ids=true | all-gather | bytes 456192 | tf_op jit(solution)/shard_map/all_gather | solution.py:62
  600.2 0.2 reshape.11
  600.4 1.1 fusion.10
  601.5 0.0 all-reduce.9.cloned.1.call-update
  601.5 0.6 copy.24
  602.2 1.2 convolution_bitcast_fusion
  603.3 178.1 %all-reduce.9.cloned.1.call-done = f32[384,256]{1,0:T(8,128)} async-done(((f32[384,256]{1,0:T(8,128)}), f32[384,256]{1,0:T(8,128)}) %all-reduce.9.cloned.1.call-update) | async-done | bytes 393232 | tf_op jit(solution)/shard_map/psum | solution.py:64
  781.4 1.8 copy.29
  (24 shorter events, 0.1 us)
Async XLA Ops:
  7.2 63.5 %copy-start = (bf16[1,576,576]{2,1,0:T(8,128)(2,1)S(1)}, bf16[1,576,576]{2,1,0:T(8,128)(2,1)}, u32[]{:S(2)}) copy-start(bf16[1,576,576]{2,1,0:T(8,128)(2,1)} %param.10) | copy-start | bytes 1990660
  7.2 114.6 %reduce-scatter.8.cloned.1.call-start = ((), (), s32[]{:S(2)}) async-start(), calls=%async_computation.3 | async-start | bytes 1990656 | tf_op jit(solution)/shard_map/reduce_scatter | solution.py:26
  70.0 1.3 copy-start.3
  74.0 64.2 %copy-start.4 = (bf16[1,576,576]{2,1,0:T(8,128)(2,1)S(1)}, bf16[1,576,576]{2,1,0:T(8,128)(2,1)}, u32[]{:S(2)}) copy-start(bf16[1,576,576]{2,1,0:T(8,128)(2,1)} %param.11) | copy-start | bytes 1990660
  74.1 386.2 %all-reduce.7.cloned.1.call-start = ((), (), s32[]{:S(2)}) async-start(), calls=%async_computation.1 | async-start | bytes 786432 | tf_op jit(solution)/shard_map/psum | solution.py:50
  138.8 140.3 %copy-start.5 = (bf16[1,576,256]{2,1,0:T(8,128)(2,1)S(1)}, bf16[1,576,256]{2,1,0:T(8,128)(2,1)}, u32[]{:S(2)}) copy-start(bf16[1,576,256]{2,1,0:T(8,128)(2,1)} %param.12) | copy-start | bytes 884740
  197.9 21.9 %collective-permute-start = (bf16[16,576]{1,0:T(8,128)(2,1)S(1)}, bf16[16,576]{1,0:T(8,128)(2,1)S(1)}, u32[]{:S(2)}, u32[]{:S(2)}) collective-permute-start(bf16[16,576]{1,0:T(8,128)(2,1)S(1)} %convert.14), channel_id=1, source_target_pairs={{0,1},{1,2},{2,3},{3,4},{4,5},{5,6},{6,7},{7,8},{8,9},{9,10},{10,1... | collective-permute-start | bytes 55304
  199.6 23.6 %collective-permute-start.1 = (bf16[16,576]{1,0:T(8,128)(2,1)S(1)}, bf16[16,576]{1,0:T(8,128)(2,1)S(1)}, u32[]{:S(2)}, u32[]{:S(2)}) collective-permute-start(bf16[16,576]{1,0:T(8,128)(2,1)S(1)} %convert.14), channel_id=1, source_target_pairs={{0,2},{1,3},{2,4},{3,5},{4,6},{5,7},{6,8},{7,9},{8,10},{9,11},{10,... | collective-permute-start | bytes 55304
  201.7 15.9 %collective-permute-start.7 = (bf16[12,576]{1,0:T(8,128)(2,1)S(1)}, bf16[12,576]{1,0:T(8,128)(2,1)S(1)}, u32[]{:S(2)}, u32[]{:S(2)}) collective-permute-start(bf16[12,576]{1,0:T(8,128)(2,1)S(1)} %slice.10), channel_id=1, source_target_pairs={{0,8},{1,9},{2,10},{3,11},{4,12},{5,13},{6,14},{7,15},{8,16},{9,17... | collective-permute-start | bytes 41480
  207.7 20.3 %collective-permute-start.2 = (bf16[16,576]{1,0:T(8,128)(2,1)S(1)}, bf16[16,576]{1,0:T(8,128)(2,1)S(1)}, u32[]{:S(2)}, u32[]{:S(2)}) collective-permute-start(bf16[16,576]{1,0:T(8,128)(2,1)S(1)} %convert.14), channel_id=1, source_target_pairs={{0,3},{1,4},{2,5},{3,6},{4,7},{5,8},{6,9},{7,10},{8,11},{9,12},{10... | collective-permute-start | bytes 55304
  212.7 15.3 %collective-permute-start.3 = (bf16[16,576]{1,0:T(8,128)(2,1)S(1)}, bf16[16,576]{1,0:T(8,128)(2,1)S(1)}, u32[]{:S(2)}, u32[]{:S(2)}) collective-permute-start(bf16[16,576]{1,0:T(8,128)(2,1)S(1)} %convert.14), channel_id=1, source_target_pairs={{0,4},{1,5},{2,6},{3,7},{4,8},{5,9},{6,10},{7,11},{8,12},{9,13},{1... | collective-permute-start | bytes 55304
  217.6 10.4 %collective-permute-start.4 = (bf16[16,576]{1,0:T(8,128)(2,1)S(1)}, bf16[16,576]{1,0:T(8,128)(2,1)S(1)}, u32[]{:S(2)}, u32[]{:S(2)}) collective-permute-start(bf16[16,576]{1,0:T(8,128)(2,1)S(1)} %convert.14), channel_id=1, source_target_pairs={{0,5},{1,6},{2,7},{3,8},{4,9},{5,10},{6,11},{7,12},{8,13},{9,14},{... | collective-permute-start | bytes 55304
  219.8 8.3 %collective-permute-start.5 = (bf16[16,576]{1,0:T(8,128)(2,1)S(1)}, bf16[16,576]{1,0:T(8,128)(2,1)S(1)}, u32[]{:S(2)}, u32[]{:S(2)}) collective-permute-start(bf16[16,576]{1,0:T(8,128)(2,1)S(1)} %convert.14), channel_id=1, source_target_pairs={{0,6},{1,7},{2,8},{3,9},{4,10},{5,11},{6,12},{7,13},{8,14},{9,15},... | collective-permute-start | bytes 55304
  223.2 4.8 collective-permute-start.6
  229.4 230.8 %copy-start.2 = (bf16[256,1,576]{0,2,1:T(8,128)(2,1)S(1)}, bf16[256,1,576]{0,2,1:T(8,128)(2,1)}, u32[]{:S(2)}) copy-start(bf16[256,1,576]{0,2,1:T(8,128)(2,1)} %param.14) | copy-start | bytes 884740
  229.4 230.8 %copy-start.6 = (f32[256]{0:T(256)S(1)}, f32[256]{0:T(256)}, u32[]{:S(2)}) copy-start(f32[256]{0:T(256)} %param.13) | copy-start | bytes 3076
  280.2 269.0 %copy-start.7 = (f32[1,576]{1,0:T(1,128)S(1)}, f32[1,576]{1,0:T(1,128)}, u32[]{:S(2)}) copy-start(f32[1,576]{1,0:T(1,128)} %param.15) | copy-start | bytes 6916
  280.2 501.2 %all-reduce.9.cloned.1.call-start = ((), (), s32[]{:S(2)}) async-start(), calls=%async_computation.2 | async-start | bytes 786432 | tf_op jit(solution)/shard_map/psum | solution.py:64
  520.7 23.1 %collective-permute-start.10 = (f32[16,576]{1,0:T(8,128)S(1)}, f32[16,576]{1,0:T(8,128)S(1)}, u32[]{:S(2)}, u32[]{:S(2)}) collective-permute-start(f32[16,576]{1,0:T(8,128)S(1)} %fusion.1), channel_id=1, source_target_pairs={{0,3},{1,4},{2,5},{3,6},{4,7},{5,8},{6,9},{7,10},{8,11},{9,12},{10... | collective-permute-start | bytes 110600
  522.0 24.9 %collective-permute-start.11 = (f32[16,576]{1,0:T(8,128)S(1)}, f32[16,576]{1,0:T(8,128)S(1)}, u32[]{:S(2)}, u32[]{:S(2)}) collective-permute-start(f32[16,576]{1,0:T(8,128)S(1)} %fusion.1), channel_id=1, source_target_pairs={{0,4},{1,5},{2,6},{3,7},{4,8},{5,9},{6,10},{7,11},{8,12},{9,13},{1... | collective-permute-start | bytes 110600
  525.5 15.5 %collective-permute-start.15 = (f32[12,576]{1,0:T(8,128)S(1)}, f32[12,576]{1,0:T(8,128)S(1)}, u32[]{:S(2)}, u32[]{:S(2)}) collective-permute-start(f32[12,576]{1,0:T(8,128)S(1)} %slice.11), channel_id=1, source_target_pairs={{0,8},{1,9},{2,10},{3,11},{4,12},{5,13},{6,14},{7,15},{8,16},{9,17... | collective-permute-start | bytes 82952
  532.6 16.7 %collective-permute-start.12 = (f32[16,576]{1,0:T(8,128)S(1)}, f32[16,576]{1,0:T(8,128)S(1)}, u32[]{:S(2)}, u32[]{:S(2)}) collective-permute-start(f32[16,576]{1,0:T(8,128)S(1)} %fusion.1), channel_id=1, source_target_pairs={{0,5},{1,6},{2,7},{3,8},{4,9},{5,10},{6,11},{7,12},{8,13},{9,14},{... | collective-permute-start | bytes 110600
  537.1 12.2 %collective-permute-start.13 = (f32[16,576]{1,0:T(8,128)S(1)}, f32[16,576]{1,0:T(8,128)S(1)}, u32[]{:S(2)}, u32[]{:S(2)}) collective-permute-start(f32[16,576]{1,0:T(8,128)S(1)} %fusion.1), channel_id=1, source_target_pairs={{0,6},{1,7},{2,8},{3,9},{4,10},{5,11},{6,12},{7,13},{8,14},{9,15},... | collective-permute-start | bytes 110600
  541.0 8.2 %collective-permute-start.14 = (f32[16,576]{1,0:T(8,128)S(1)}, f32[16,576]{1,0:T(8,128)S(1)}, u32[]{:S(2)}, u32[]{:S(2)}) collective-permute-start(f32[16,576]{1,0:T(8,128)S(1)} %fusion.1), channel_id=1, source_target_pairs={{0,7},{1,8},{2,9},{3,10},{4,11},{5,12},{6,13},{7,14},{8,15},{9,16}... | collective-permute-start | bytes 110600
  543.9 5.4 collective-permute-start.8
  547.0 3.3 collective-permute-start.9
  551.3 50.8 %copy-start.1 = (f32[384,256]{1,0:T(8,128)S(1)}, f32[384,256]{1,0:T(8,128)}, u32[]{:S(2)}) copy-start(f32[384,256]{1,0:T(8,128)} %all-reduce.7.cloned.1.call-done) | copy-start | bytes 1179652
Sparse Core Ops, SparseCore 0:
  74.2 47.5 reduce-scatter.7
  280.3 179.8 all-reduce.6
  601.6 179.7 all-reduce.8
where the time goes:
time: 790 us
  waiting for transfers between devices  407 us (52%)
  blocking collectives  294 us (37%)
  starting transfers between devices  56.6 us (7%)
  between operations  14.9 us (2%)
  local copies, waits for them, and re-layouts  10 us (1%)
    psum x1, waiting for transfers between devices, body(): pre = lax.psum(partial_pre, ('mp', 'tok'))  180 us
    psum x1, waiting for transfers between devices, body(): latent_grad = lax.psum(contract_cols(error_all, decoder), ('mp', 'tok'))  178 us
    unnamed x2, blocking collectives  118 us
    all_gather x1, blocking collectives, body(): gathered = lax.all_gather(x_rows, 'lat', axis=0, tiled=True)  61.9 us
    unnamed x16, starting transfers between devices  56.5 us
    all_gather x1, blocking collectives, body(): acts_all = lax.all_gather(acts, 'lat', axis=0, tiled=True)  49.4 us
    all_gather x1, blocking collectives, body(): lax.all_gather(error.astype(jnp.bfloat16), 'lat', axis=0, tiled=True)  48.9 us
    reduce_scatter x1, waiting for transfers between devices, body(): lax.psum_scatter(jnp.concatenate([jnp.dot(block, gate_local, preferred_el...  47.7 us
  transfers between devices with their start and end apart: 19, of which 4 were waited for; matrix products, arithmetic and copies ran while one was open for 0% of the time, Pallas kernels for 0%

commit v1 on v0

--- a/solution.py
+++ b/solution.py
@@ -61,7 +61,7 @@
     error = recon + bias_row - acts.astype(jnp.float32)
     error_all = lax.all_gather(error.astype(jnp.bfloat16), "lat", axis=0, tiled=True)
     decoder_grad = contract_rows(codes, error_all)
-    latent_grad = lax.psum(contract_cols(error_all, decoder), ("mp", "tok"))
+    latent_grad = lax.psum(lax.psum(contract_cols(error_all, decoder), "tok"), "mp")
     return (error[None], decoder_grad[:, None, :], latent_grad)
 
 

time: 790 us -> 764 us (0.967)
  waiting for transfers between devices: 407 us -> 380 us
    psum x1 -> x2, waiting for transfers between devices: 178 us -> 151 us  [the longest x1 101 us: body(): lax.psum(contract_cols(error_all, decoder), 'tok')]
  transfers between devices with their start and end apart: 19 -> 20, of which waited for: 4 -> 5; matrix products, arithmetic and copies ran while one was open for 0% -> 0% of each run, Pallas kernels for 0% -> 0%
where the time goes in v1:
time: 764 us; the launch traced here: 763 us
  waiting for transfers between devices  380 us (50%)
  blocking collectives  294 us (38%)
  starting transfers between devices  56.6 us (7%)
  between operations  14.9 us (2%)
  local copies, waits for them, and re-layouts  10 us (1%)
    psum x1, waiting for transfers between devices, body(): pre = lax.psum(partial_pre, ('mp', 'tok'))  180 us
    unnamed x2, blocking collectives  118 us
    psum x1, waiting for transfers between devices, body(): lax.psum(contract_cols(error_all, decoder), 'tok')  101 us
    all_gather x1, blocking collectives, body(): gathered = lax.all_gather(x_rows, 'lat', axis=0, tiled=True)  61.9 us
    unnamed x16, starting transfers between devices  56.5 us
    psum x1, waiting for transfers between devices, body(): lax.psum(lax.psum(contract_cols(error_all, decoder), 'tok'), 'mp')  50.9 us
    all_gather x1, blocking collectives, body(): acts_all = lax.all_gather(acts, 'lat', axis=0, tiled=True)  49.4 us
    all_gather x1, blocking collectives, body(): lax.all_gather(error.astype(jnp.bfloat16), 'lat', axis=0, tiled=True)  48.9 us
  transfers between devices with their start and end apart: 20, of which 5 were waited for; matrix products, arithmetic and copies ran while one was open for 0% of the time, Pallas kernels for 0%

profile of v1, /device:TPU:1, one launch (start us, length us, event | category | flops | bytes accessed | tf_op | source)
XLA Modules:
  0.0 763.2 jit_solution(16426075653769772184)
XLA Ops:
  7.2 0.0 copy-start
  7.2 0.0 reduce-scatter.8.cloned.1.call-start
  7.2 0.8 copy.20
  8.0 61.9 %all-gather = bf16[1,384,576]{2,0,1:T(2,128)(2,1)S(1)} all-gather(bf16[1,12,576]{2,0,1:T(2,128)(2,1)S(1)} %copy.20), channel_id=2, replica_groups=mesh['mp'=2,'tok'=8,'lat'=32] {'lat'}, dimensions={1}, use_global_device_ids=true | all-gather | bytes 456192 | tf_op jit(solution)/shard_map/all_gather | solution.py:21
  70.0 0.7 copy.21
  70.6 0.6 fusion.4
  71.3 0.6 fusion.6
  71.9 0.1 pad_maximum_fusion
  72.1 2.0 copy.25
  74.0 0.0 reduce-scatter.8.cloned.1.call-update
  74.1 0.0 all-reduce.8.cloned.1.call-start
  74.1 47.7 %reduce-scatter.8.cloned.1.call-done = f32[48,1152]{1,0:T(8,128)} async-done(((f32[384,1152]{1,0:T(8,128)}), f32[48,1152]{1,0:T(8,128)}) %reduce-scatter.8.cloned.1.call-update) | async-done | bytes 221200 | tf_op jit(solution)/shard_map/reduce_scatter | solution.py:26
  121.8 1.1 fusion.24
  122.9 15.4 %all_gather.13 = bf16[384,576]{1,0:T(8,128)(2,1)S(1)} all-gather(bf16[48,576]{1,0:T(8,128)(2,1)S(1)} %fusion.24), channel_id=1, replica_groups=mesh['mp'=2,'tok'=8,'lat'=32] {'tok'}, dimensions={0}, use_global_device_ids=true | all-gather | bytes 497664 | tf_op jit(solution)/shard_map/all_gather | solution.py:39
  138.2 0.6 fusion.2
  138.8 0.0 copy-start.5
  138.8 59.0 %fusion = f32[16,576]{1,0:T(8,128)S(1)} fusion(f32[384,576]{1,0:T(8,128)S(1)} %fusion.2), kind=kCustom, calls=%all-reduce-scatter | all-reduce-scatter fusion | flops 294913 | bytes 923648
  197.9 1.7 collective-permute-start
  199.6 2.1 collective-permute-start.1
  201.7 6.0 collective-permute-start.7
  207.7 4.9 collective-permute-start.2
  212.7 4.9 collective-permute-start.3
  217.6 0.0 collective-permute-done.7
  217.6 2.1 collective-permute-start.4
  219.8 3.5 collective-permute-start.5
  223.2 0.0 collective-permute-done.1
  223.2 2.8 collective-permute-start.6
  226.1 1.3 dynamic-slice.6
  228.0 0.0 collective-permute-done.2
  228.0 0.0 collective-permute-done.4
  228.0 0.0 collective-permute-done.5
  228.1 1.3 concatenate.4
  229.4 0.0 copy-start.2
  229.4 0.0 copy-start.6
  229.4 49.4 %all-gather.1 = bf16[32,12,576]{2,1,0:T(8,128)(2,1)S(1)} all-gather(bf16[1,12,576]{2,1,0:T(8,128)(2,1)S(1)} %fusion.31), channel_id=1, replica_groups=mesh['mp'=2,'tok'=8,'lat'=32] {'lat'}, dimensions={0}, use_global_device_ids=true | all-gather | bytes 456192 | tf_op jit(solution)/shard_map/all_gather | solution.py:48
  278.8 0.2 reshape.9
  279.1 1.1 fusion.14
  280.2 0.0 all-reduce.8.cloned.1.call-update
  280.2 0.0 all-reduce.10.cloned.1.call-start
  280.2 180.0 %all-reduce.8.cloned.1.call-done = f32[384,256]{1,0:T(8,128)} async-done(((f32[384,256]{1,0:T(8,128)}), f32[384,256]{1,0:T(8,128)}) %all-reduce.8.cloned.1.call-update) | async-done | bytes 393232 | tf_op jit(solution)/shard_map/psum | solution.py:50
  460.2 1.3 fusion.12
  461.6 59.2 %fusion.1 = f32[16,576]{1,0:T(8,128)S(1)} fusion(f32[384,576]{1,0:T(8,128)S(1)} %fusion.12), kind=kCustom, calls=%all-reduce-scatter.1 | all-reduce-scatter fusion | flops 294913 | bytes 923648
  520.7 1.3 collective-permute-start.10
  522.0 3.4 collective-permute-start.11
  525.5 7.0 collective-permute-start.15
  532.6 4.5 collective-permute-start.12
  537.1 3.9 collective-permute-start.13
  541.0 0.0 collective-permute-done.15
  541.0 2.9 collective-permute-start.14
  543.9 3.1 collective-permute-start.8
  547.0 2.2 collective-permute-start.9
  549.3 1.0 collective-permute-done.9
  550.3 1.0 concatenate.5
  551.3 48.9 %all-gather.2 = bf16[32,12,576]{2,1,0:T(8,128)(2,1)S(1)} all-gather(bf16[1,12,576]{2,1,0:T(8,128)(2,1)S(1)} %get-tuple-element.18), channel_id=1, replica_groups=mesh['mp'=2,'tok'=8,'lat'=32] {'lat'}, dimensions={0}, use_global_device_ids=true | all-gather | bytes 456192 | tf_op jit(solution)/shard_map/all_gather | solution.py:62
  600.2 0.2 reshape.11
  600.4 1.1 fusion.10
  601.5 0.0 all-reduce.10.cloned.1.call-update
  601.5 0.0 all-reduce.12.cloned.1.call-start
  601.6 100.6 %all-reduce.10.cloned.1.call-done = f32[384,256]{1,0:T(8,128)} async-done(((f32[384,256]{1,0:T(8,128)}), f32[384,256]{1,0:T(8,128)}) %all-reduce.10.cloned.1.call-update) | async-done | bytes 393232 | tf_op jit(solution)/shard_map/psum | solution.py:64
  702.2 0.0 all-reduce.12.cloned.1.call-update
  702.2 0.6 copy.24
  702.8 1.2 convolution_bitcast_fusion
  704.0 50.9 %all-reduce.12.cloned.1.call-done = f32[384,256]{1,0:T(8,128)} async-done(((f32[384,256]{1,0:T(8,128)}), f32[384,256]{1,0:T(8,128)}) %all-reduce.12.cloned.1.call-update) | async-done | bytes 393232 | tf_op jit(solution)/shard_map/psum | solution.py:64
  754.9 1.8 copy.30
  (27 shorter events, 0.1 us)
Async XLA Ops:
  7.2 63.5 %copy-start = (bf16[1,576,576]{2,1,0:T(8,128)(2,1)S(1)}, bf16[1,576,576]{2,1,0:T(8,128)(2,1)}, u32[]{:S(2)}) copy-start(bf16[1,576,576]{2,1,0:T(8,128)(2,1)} %param.10) | copy-start | bytes 1990660
  7.2 114.6 %reduce-scatter.8.cloned.1.call-start = ((), (), s32[]{:S(2)}) async-start(), calls=%async_computation.4 | async-start | bytes 1990656 | tf_op jit(solution)/shard_map/reduce_scatter | solution.py:26
  70.0 1.3 copy-start.3
  74.0 64.2 %copy-start.4 = (bf16[1,576,576]{2,1,0:T(8,128)(2,1)S(1)}, bf16[1,576,576]{2,1,0:T(8,128)(2,1)}, u32[]{:S(2)}) copy-start(bf16[1,576,576]{2,1,0:T(8,128)(2,1)} %param.11) | copy-start | bytes 1990660
  74.1 386.2 %all-reduce.8.cloned.1.call-start = ((), (), s32[]{:S(2)}) async-start(), calls=%async_computation.1 | async-start | bytes 786432 | tf_op jit(solution)/shard_map/psum | solution.py:50
  138.8 140.3 %copy-start.5 = (bf16[1,576,256]{2,1,0:T(8,128)(2,1)S(1)}, bf16[1,576,256]{2,1,0:T(8,128)(2,1)}, u32[]{:S(2)}) copy-start(bf16[1,576,256]{2,1,0:T(8,128)(2,1)} %param.12) | copy-start | bytes 884740
  197.9 21.9 %collective-permute-start = (bf16[16,576]{1,0:T(8,128)(2,1)S(1)}, bf16[16,576]{1,0:T(8,128)(2,1)S(1)}, u32[]{:S(2)}, u32[]{:S(2)}) collective-permute-start(bf16[16,576]{1,0:T(8,128)(2,1)S(1)} %convert.14), channel_id=1, source_target_pairs={{0,1},{1,2},{2,3},{3,4},{4,5},{5,6},{6,7},{7,8},{8,9},{9,10},{10,1... | collective-permute-start | bytes 55304
  199.6 23.6 %collective-permute-start.1 = (bf16[16,576]{1,0:T(8,128)(2,1)S(1)}, bf16[16,576]{1,0:T(8,128)(2,1)S(1)}, u32[]{:S(2)}, u32[]{:S(2)}) collective-permute-start(bf16[16,576]{1,0:T(8,128)(2,1)S(1)} %convert.14), channel_id=1, source_target_pairs={{0,2},{1,3},{2,4},{3,5},{4,6},{5,7},{6,8},{7,9},{8,10},{9,11},{10,... | collective-permute-start | bytes 55304
  201.7 15.9 %collective-permute-start.7 = (bf16[12,576]{1,0:T(8,128)(2,1)S(1)}, bf16[12,576]{1,0:T(8,128)(2,1)S(1)}, u32[]{:S(2)}, u32[]{:S(2)}) collective-permute-start(bf16[12,576]{1,0:T(8,128)(2,1)S(1)} %slice.10), channel_id=1, source_target_pairs={{0,8},{1,9},{2,10},{3,11},{4,12},{5,13},{6,14},{7,15},{8,16},{9,17... | collective-permute-start | bytes 41480
  207.7 20.3 %collective-permute-start.2 = (bf16[16,576]{1,0:T(8,128)(2,1)S(1)}, bf16[16,576]{1,0:T(8,128)(2,1)S(1)}, u32[]{:S(2)}, u32[]{:S(2)}) collective-permute-start(bf16[16,576]{1,0:T(8,128)(2,1)S(1)} %convert.14), channel_id=1, source_target_pairs={{0,3},{1,4},{2,5},{3,6},{4,7},{5,8},{6,9},{7,10},{8,11},{9,12},{10... | collective-permute-start | bytes 55304
  212.7 15.3 %collective-permute-start.3 = (bf16[16,576]{1,0:T(8,128)(2,1)S(1)}, bf16[16,576]{1,0:T(8,128)(2,1)S(1)}, u32[]{:S(2)}, u32[]{:S(2)}) collective-permute-start(bf16[16,576]{1,0:T(8,128)(2,1)S(1)} %convert.14), channel_id=1, source_target_pairs={{0,4},{1,5},{2,6},{3,7},{4,8},{5,9},{6,10},{7,11},{8,12},{9,13},{1... | collective-permute-start | bytes 55304
  217.6 10.4 %collective-permute-start.4 = (bf16[16,576]{1,0:T(8,128)(2,1)S(1)}, bf16[16,576]{1,0:T(8,128)(2,1)S(1)}, u32[]{:S(2)}, u32[]{:S(2)}) collective-permute-start(bf16[16,576]{1,0:T(8,128)(2,1)S(1)} %convert.14), channel_id=1, source_target_pairs={{0,5},{1,6},{2,7},{3,8},{4,9},{5,10},{6,11},{7,12},{8,13},{9,14},{... | collective-permute-start | bytes 55304
  219.8 8.3 %collective-permute-start.5 = (bf16[16,576]{1,0:T(8,128)(2,1)S(1)}, bf16[16,576]{1,0:T(8,128)(2,1)S(1)}, u32[]{:S(2)}, u32[]{:S(2)}) collective-permute-start(bf16[16,576]{1,0:T(8,128)(2,1)S(1)} %convert.14), channel_id=1, source_target_pairs={{0,6},{1,7},{2,8},{3,9},{4,10},{5,11},{6,12},{7,13},{8,14},{9,15},... | collective-permute-start | bytes 55304
  223.2 4.8 collective-permute-start.6
  229.4 230.8 %copy-start.2 = (bf16[256,1,576]{0,2,1:T(8,128)(2,1)S(1)}, bf16[256,1,576]{0,2,1:T(8,128)(2,1)}, u32[]{:S(2)}) copy-start(bf16[256,1,576]{0,2,1:T(8,128)(2,1)} %param.14) | copy-start | bytes 884740
  229.4 230.8 %copy-start.6 = (f32[256]{0:T(256)S(1)}, f32[256]{0:T(256)}, u32[]{:S(2)}) copy-start(f32[256]{0:T(256)} %param.13) | copy-start | bytes 3076
  280.2 269.0 %copy-start.7 = (f32[1,576]{1,0:T(1,128)S(1)}, f32[1,576]{1,0:T(1,128)}, u32[]{:S(2)}) copy-start(f32[1,576]{1,0:T(1,128)} %param.15) | copy-start | bytes 6916
  280.2 422.0 %all-reduce.10.cloned.1.call-start = ((), (), s32[]{:S(2)}) async-start(), calls=%async_computation.2 | async-start | bytes 786432 | tf_op jit(solution)/shard_map/psum | solution.py:64
  520.7 23.1 %collective-permute-start.10 = (f32[16,576]{1,0:T(8,128)S(1)}, f32[16,576]{1,0:T(8,128)S(1)}, u32[]{:S(2)}, u32[]{:S(2)}) collective-permute-start(f32[16,576]{1,0:T(8,128)S(1)} %fusion.1), channel_id=1, source_target_pairs={{0,3},{1,4},{2,5},{3,6},{4,7},{5,8},{6,9},{7,10},{8,11},{9,12},{10... | collective-permute-start | bytes 110600
  522.0 24.9 %collective-permute-start.11 = (f32[16,576]{1,0:T(8,128)S(1)}, f32[16,576]{1,0:T(8,128)S(1)}, u32[]{:S(2)}, u32[]{:S(2)}) collective-permute-start(f32[16,576]{1,0:T(8,128)S(1)} %fusion.1), channel_id=1, source_target_pairs={{0,4},{1,5},{2,6},{3,7},{4,8},{5,9},{6,10},{7,11},{8,12},{9,13},{1... | collective-permute-start | bytes 110600
  525.5 15.5 %collective-permute-start.15 = (f32[12,576]{1,0:T(8,128)S(1)}, f32[12,576]{1,0:T(8,128)S(1)}, u32[]{:S(2)}, u32[]{:S(2)}) collective-permute-start(f32[12,576]{1,0:T(8,128)S(1)} %slice.11), channel_id=1, source_target_pairs={{0,8},{1,9},{2,10},{3,11},{4,12},{5,13},{6,14},{7,15},{8,16},{9,17... | collective-permute-start | bytes 82952
  532.6 16.7 %collective-permute-start.12 = (f32[16,576]{1,0:T(8,128)S(1)}, f32[16,576]{1,0:T(8,128)S(1)}, u32[]{:S(2)}, u32[]{:S(2)}) collective-permute-start(f32[16,576]{1,0:T(8,128)S(1)} %fusion.1), channel_id=1, source_target_pairs={{0,5},{1,6},{2,7},{3,8},{4,9},{5,10},{6,11},{7,12},{8,13},{9,14},{... | collective-permute-start | bytes 110600
  537.1 12.2 %collective-permute-start.13 = (f32[16,576]{1,0:T(8,128)S(1)}, f32[16,576]{1,0:T(8,128)S(1)}, u32[]{:S(2)}, u32[]{:S(2)}) collective-permute-start(f32[16,576]{1,0:T(8,128)S(1)} %fusion.1), channel_id=1, source_target_pairs={{0,6},{1,7},{2,8},{3,9},{4,10},{5,11},{6,12},{7,13},{8,14},{9,15},... | collective-permute-start | bytes 110600
  541.0 8.2 %collective-permute-start.14 = (f32[16,576]{1,0:T(8,128)S(1)}, f32[16,576]{1,0:T(8,128)S(1)}, u32[]{:S(2)}, u32[]{:S(2)}) collective-permute-start(f32[16,576]{1,0:T(8,128)S(1)} %fusion.1), channel_id=1, source_target_pairs={{0,7},{1,8},{2,9},{3,10},{4,11},{5,12},{6,13},{7,14},{8,15},{9,16}... | collective-permute-start | bytes 110600
  543.9 5.4 collective-permute-start.8
  547.0 3.3 collective-permute-start.9
  551.3 151.5 %copy-start.1 = (f32[384,256]{1,0:T(8,128)S(1)}, f32[384,256]{1,0:T(8,128)}, u32[]{:S(2)}) copy-start(f32[384,256]{1,0:T(8,128)} %all-reduce.8.cloned.1.call-done) | copy-start | bytes 1179652
  601.5 153.4 %all-reduce.12.cloned.1.call-start = ((), (), s32[]{:S(2)}) async-start(), calls=%async_computation.3 | async-start | bytes 786432 | tf_op jit(solution)/shard_map/psum | solution.py:64
Sparse Core Ops, SparseCore 0:
  74.2 47.5 reduce-scatter.7
  280.3 179.8 all-reduce.7
  601.6 100.4 all-reduce.9
  704.9 49.9 all-reduce.11
